TPU v7x, 128 devices: a whole 4x4x4 slice. The times are simulated.
128 devices in a mesh: dp: 32 (over x, z, y_lo), mp: 4 (over y_hi, core).
Axes of the slice: x: 4, y: 4 (y_hi: 2, y_lo: 2; y = y_hi * 2 + y_lo), z: 4, core: 2. Of those that a mesh axis runs over, the one named last changes fastest.
Arguments:
- inputs: bfloat16 [12288, 8192], P('dp', 'mp'), may hold values from -6 to 6
- gate_preact: bfloat16 [12288, 28672], P('dp', 'mp'), may hold values from -6 to 6
- hidden_grad: bfloat16 [12288, 28672], P('dp', 'mp'), may hold values from -0.109375 to 0.109375
- projector: bfloat16 [8192, 512], P('mp'), may hold values from -0.0625 to 0.0625
- first_moment: float32 [28672, 512], P(('mp', 'dp')), may hold values from -0.6 to 0.6
- second_moment: float32 [28672, 512], P(('mp', 'dp')), may hold values from 0.01 to 0.1
Outputs:
- new_first: float32 [28672, 512], P(('mp', 'dp'))
- new_second: float32 [28672, 512], P(('mp', 'dp'))
- weight_update: bfloat16 [28672, 8192], P(('mp', 'dp'))
All inputs are finite; a program needn't handle non-finite values.
Results may differ from a plain program's by a relative error of at most 0.0058.
Values may be sent and summed in bfloat16 or wider, within the bound.
No kernel may reach another device: no remote copies, remote signals or barrier semaphores. Data moves between devices by JAX's collectives and lax.ppermute only.
A program may use at most 128 MiB of HBM per device.

v0:
```python
import jax
import jax.numpy as jnp
from jax import lax
from jax.sharding import PartitionSpec as P


def local(inputs, gate_preact, hidden_grad, projector, first_moment, second_moment):
    grad_up = (
        hidden_grad.astype(jnp.float32) * jax.nn.silu(gate_preact.astype(jnp.float32))
    ).astype(jnp.bfloat16)
    full_proj = lax.all_gather(projector, "mp", axis=0, tiled=True)
    coord_sum = jnp.dot(
        lax.all_gather(inputs, "mp", axis=1, tiled=True),
        full_proj,
        preferred_element_type=jnp.float32,
    )
    coords = coord_sum.astype(jnp.bfloat16)
    projected = lax.psum_scatter(
        lax.dot_general(
            grad_up, coords, (((0,), (0,)), ((), ())), preferred_element_type=jnp.float32
        ),
        "dp",
        scatter_dimension=0,
        tiled=True,
    )
    new_first = 0.9 * first_moment + 0.1 * projected
    new_second = 0.95 * second_moment + 0.05 * projected * projected
    direction = new_first / (1.0 - 0.81) / (jnp.sqrt(new_second / (1.0 - 0.9025)) + 1e-08)
    direction = direction.astype(jnp.bfloat16)
    update = 4.0 * lax.dot_general(
        direction, full_proj, (((1,), (1,)), ((), ())), preferred_element_type=jnp.float32
    )
    return (new_first, new_second, update.astype(jnp.bfloat16))


def solution(mesh):
    return jax.shard_map(
        local,
        mesh=mesh,
        in_specs=(
            P("dp", "mp"),
            P("dp", "mp"),
            P("dp", "mp"),
            P("mp", None),
            P(("mp", "dp"), None),
            P(("mp", "dp"), None),
        ),
        out_specs=(P(("mp", "dp"), None), P(("mp", "dp"), None), P(("mp", "dp"), None)),
        check_vma=False,
    )
```

profile of v0, /device:TPU:74, one launch (start us, length us, event | category | flops | bytes accessed | tf_op | source)
XLA Modules:
  0.0 480.9 jit_solution(11658029528777716738)
XLA Ops:
  7.2 0.0 all-gather.3.cloned.1.call-start
  7.2 0.7 all-gather.3.cloned.1.call-update
  7.9 0.0 all-gather.5.cloned.1.call-start
  7.9 0.7 all-gather.5.cloned.1.call-update
  8.6 0.0 reduce-scatter.2.cloned.1.call-start
  8.7 52.0 %all-gather.3.cloned.1.call-done = bf16[384,8192]{1,0:T(8,128)(2,1)} async-done(((bf16[384,2048]{1,0:T(8,128)(2,1)}), bf16[384,8192]{1,0:T(8,128)(2,1)}) %all-gather.3.cloned.1.call-update) | async-done | bytes 6291472 | tf_op jit(solution)/shard_map/all_gather | solution.py:13
  60.7 63.4 %all-gather.5.cloned.1.call-done = bf16[8192,512]{1,0:T(8,128)(2,1)} async-done(((bf16[2048,512]{1,0:T(8,128)(2,1)}), bf16[8192,512]{1,0:T(8,128)(2,1)}) %all-gather.5.cloned.1.call-update) | async-done | bytes 8388624 | tf_op jit(solution)/shard_map/all_gather | solution.py:11
  124.1 21.4 %fusion.6 = f32[7168,512]{1,0:T(8,128)} fusion(bf16[384,7168]{1,0:T(8,128)(2,1)} %param.7, bf16[384,7168]{1,0:T(8,128)(2,1)} %param.8, bf16[384,8192]{1,0:T(8,128)(2,1)} %all-gather.3.cloned.1.call-done, bf16[8192,512]{1,0:T(8,128)(2,1)} %all-gather.5.cloned.1.call-done), kind=kOutput, calls=%fused_computation.9 | convolution fusion | flops 6062014464 | bytes 40370176 | tf_op jit(solution)/shard_map/dot_general | solution.py:19
  145.5 0.0 copy-start
  145.5 0.0 copy-start.1
  145.5 0.0 reduce-scatter.2.cloned.1.call-update
  145.5 319.3 %reduce-scatter.2.cloned.1.call-done = f32[224,512]{1,0:T(8,128)} async-done(((f32[7168,512]{1,0:T(8,128)}), f32[224,512]{1,0:T(8,128)}) %reduce-scatter.2.cloned.1.call-update) | async-done | bytes 458768 | tf_op jit(solution)/shard_map/reduce_scatter | solution.py:18
  464.8 0.0 copy-done
  464.8 0.0 copy-done.1
  464.8 1.2 fusion.8
  466.0 0.0 copy-start.2
  466.0 0.0 copy-start.3
  466.0 8.3 %fusion.5 = bf16[224,8192]{1,0:T(8,128)(2,1)} fusion(bf16[8192,512]{1,0:T(8,128)(2,1)} %all-gather.5.cloned.1.call-done, f32[224,512]{1,0:T(8,128)S(1)} %get-tuple-element.3, f32[224,512]{1,0:T(8,128)S(1)} %get-tuple-element.4), kind=kOutput, calls=%fused_computation.8 | convolution fusion | flops 1883291648 | bytes 12976128 | tf_op jit(solution)/shard_map/dot_general | solution.py:30
  474.3 0.0 copy-done.2
  474.3 0.0 copy-done.3
Async XLA Ops:
  7.2 53.6 %all-gather.3.cloned.1.call-start = ((), (), s32[]{:S(2)}) async-start(), calls=%async_computation.1 | async-start | bytes 7864320 | tf_op jit(solution)/shard_map/all_gather | solution.py:13
  7.9 116.2 %all-gather.5.cloned.1.call-start = ((), (), s32[]{:S(2)}) async-start(), calls=%async_computation.2 | async-start | bytes 10485760 | tf_op jit(solution)/shard_map/all_gather | solution.py:11
  8.6 456.1 %reduce-scatter.2.cloned.1.call-start = ((), (), s32[]{:S(2)}) async-start(), calls=%async_computation.3 | async-start | bytes 15138816 | tf_op jit(solution)/shard_map/reduce_scatter | solution.py:18
  145.5 319.3 %copy-start = (f32[224,512]{1,0:T(8,128)S(1)}, f32[224,512]{1,0:T(8,128)}, u32[]{:S(2)}) copy-start(f32[224,512]{1,0:T(8,128)} %param.11) | copy-start | bytes 1376260
  145.5 319.3 %copy-start.1 = (f32[224,512]{1,0:T(8,128)S(1)}, f32[224,512]{1,0:T(8,128)}, u32[]{:S(2)}) copy-start(f32[224,512]{1,0:T(8,128)} %param.10) | copy-start | bytes 1376260
  466.0 8.4 %copy-start.2 = (f32[224,512]{1,0:T(8,128)}, f32[224,512]{1,0:T(8,128)S(1)}, u32[]{:S(2)}) copy-start(f32[224,512]{1,0:T(8,128)S(1)} %get-tuple-element.3) | copy-start | bytes 1376260
  466.0 8.3 %copy-start.3 = (f32[224,512]{1,0:T(8,128)}, f32[224,512]{1,0:T(8,128)S(1)}, u32[]{:S(2)}) copy-start(f32[224,512]{1,0:T(8,128)S(1)} %get-tuple-element.4) | copy-start | bytes 1376260
Sparse Core Ops, SparseCore 0:
  9.6 51.0 all-gather.2
  62.4 61.6 all-gather.4
  145.6 319.0 reduce-scatter.1
where the time goes:
time: 481 us
  waiting for transfers between devices  436 us (91%)
  matrix products  29.7 us (6%)
  between operations  13.8 us (3%)
    reduce_scatter x1, waiting for transfers between devices, local(): lax.psum_scatter(lax.dot_general(grad_up, coords, (((0,), (0,)), ((), ())...  319 us
    all_gather x1, waiting for transfers between devices, local(): full_proj = lax.all_gather(projector, 'mp', axis=0, tiled=True)  63.4 us
    all_gather x1, waiting for transfers between devices, local(): lax.all_gather(inputs, 'mp', axis=1, tiled=True)  52 us
    dot_general x1, matrix products, local(): lax.dot_general(grad_up, coords, (((0,), (0,)), ((), ())), preferred_elem...  21.4 us
  transfers between devices with their start and end apart: 3, of which 3 were waited for; matrix products, arithmetic and copies ran while one was open for 0% of the time, Pallas kernels for 0%

commit v1 on v0

--- a/solution.py
+++ b/solution.py
@@ -2,13 +2,18 @@
 import jax.numpy as jnp
 from jax import lax
 from jax.sharding import PartitionSpec as P
+from jax.lax import all_to_all, psum
+
+touch_the_classes = lambda a0: jnp.concatenate(
+    all_to_all(jnp.stack(psum(1, "mp") * [a0], axis=0), "mp", 0, 0), 0
+)
 
 
 def local(inputs, gate_preact, hidden_grad, projector, first_moment, second_moment):
     grad_up = (
         hidden_grad.astype(jnp.float32) * jax.nn.silu(gate_preact.astype(jnp.float32))
     ).astype(jnp.bfloat16)
-    full_proj = lax.all_gather(projector, "mp", axis=0, tiled=True)
+    full_proj = touch_the_classes(projector)
     coord_sum = jnp.dot(
         lax.all_gather(inputs, "mp", axis=1, tiled=True),
         full_proj,

time: 481 us -> 499 us (1.037)
  blocking collectives: 0 us -> 132 us
  waiting for transfers between devices: 436 us -> 320 us
    all_to_all x0 -> x1, blocking collectives: none -> 132 us  [all_to_all(jnp.stack(psum(1, 'mp') * [a0], axis=0), 'mp', 0, 0)]
    all_gather x1 -> x0, waiting for transfers between devices: 63.4 us -> none  [local(): full_proj = lax.all_gather(projector, 'mp', axis=0, tiled=True)]
    all_gather x1, waiting for transfers between devices: 52 us -> 0.01 us  [local(): lax.all_gather(inputs, 'mp', axis=1, tiled=True)]
  transfers between devices with their start and end apart: 3 -> 2, of which waited for: 3 -> 1; matrix products, arithmetic and copies ran while one was open for 0% -> 0% of each run, Pallas kernels for 0% -> 0%
where the time goes in v1:
time: 499 us
  waiting for transfers between devices  320 us (64%)
  blocking collectives  132 us (26%)
  matrix products  29.7 us (6%)
  between operations  14.1 us (3%)
    reduce_scatter x1, waiting for transfers between devices, local(): lax.psum_scatter(lax.dot_general(grad_up, coords, (((0,), (0,)), ((), ())...  319 us
    all_to_all x1, blocking collectives, all_to_all(jnp.stack(psum(1, 'mp') * [a0], axis=0), 'mp', 0, 0)  132 us
    dot_general x1, matrix products, local(): lax.dot_general(grad_up, coords, (((0,), (0,)), ((), ())), preferred_elem...  21.4 us
  transfers between devices with their start and end apart: 2, of which 1 were waited for; matrix products, arithmetic and copies ran while one was open for 0% of the time, Pallas kernels for 0%

profile of v1, /device:TPU:74, one launch (start us, length us, event | category | flops | bytes accessed | tf_op | source)
XLA Modules:
  0.0 498.9 jit_solution(9497055564627135242)
XLA Ops:
  7.2 0.0 all-gather.2.cloned.1.call-start
  7.2 0.7 all-gather.2.cloned.1.call-update
  7.9 0.0 reduce-scatter.2.cloned.1.call-start
  7.9 2.3 stack.2
  10.2 132.0 %all_to_all.5 = bf16[4,2048,512]{2,1,0:T(8,128)(2,1)} all-to-all(bf16[4,2048,512]{2,1,0:T(8,128)(2,1)S(1)} %stack.2), channel_id=1, replica_groups=mesh['dp'=32,'mp'=4] {'mp'}, dimensions={0} | all-to-all | bytes 16777216 | tf_op jit(solution)/shard_map/all_to_all | solution.py:8
  142.2 0.0 all-gather.2.cloned.1.call-done
  142.2 21.4 %fusion.6 = f32[7168,512]{1,0:T(8,128)} fusion(bf16[384,7168]{1,0:T(8,128)(2,1)} %param.7, bf16[384,7168]{1,0:T(8,128)(2,1)} %param.8, bf16[384,8192]{1,0:T(8,128)(2,1)} %all-gather.2.cloned.1.call-done, bf16[8192,512]{1,0:T(8,128)(2,1)} %bitcast.4), kind=kOutput, calls=%fused_computation.9 | convolution fusion | flops 6062014464 | bytes 40370176 | tf_op jit(solution)/shard_map/dot_general | solution.py:24
  163.6 0.0 copy-start
  163.6 0.0 copy-start.1
  163.6 0.0 reduce-scatter.2.cloned.1.call-update
  163.6 318.9 %reduce-scatter.2.cloned.1.call-done = f32[224,512]{1,0:T(8,128)} async-done(((f32[7168,512]{1,0:T(8,128)}), f32[224,512]{1,0:T(8,128)}) %reduce-scatter.2.cloned.1.call-update) | async-done | bytes 458768 | tf_op jit(solution)/shard_map/reduce_scatter | solution.py:23
  482.5 0.0 copy-done
  482.5 0.0 copy-done.1
  482.5 1.2 fusion.8
  483.7 0.0 copy-start.2
  483.7 0.0 copy-start.3
  483.7 8.3 %fusion.5 = bf16[224,8192]{1,0:T(8,128)(2,1)} fusion(bf16[8192,512]{1,0:T(8,128)(2,1)} %bitcast.5, f32[224,512]{1,0:T(8,128)S(1)} %get-tuple-element.3, f32[224,512]{1,0:T(8,128)S(1)} %get-tuple-element.4), kind=kOutput, calls=%fused_computation.8 | convolution fusion | flops 1883291648 | bytes 12976128 | tf_op jit(solution)/shard_map/dot_general | solution.py:35
  492.0 0.0 copy-done.2
  492.0 0.0 copy-done.3
Async XLA Ops:
  7.2 135.1 %all-gather.2.cloned.1.call-start = ((), (), s32[]{:S(2)}) async-start(), calls=%async_computation.2 | async-start | bytes 7864320 | tf_op jit(solution)/shard_map/all_gather | solution.py:18
  7.9 474.6 %reduce-scatter.2.cloned.1.call-start = ((), (), s32[]{:S(2)}) async-start(), calls=%async_computation.3 | async-start | bytes 15138816 | tf_op jit(solution)/shard_map/reduce_scatter | solution.py:23
  163.6 318.9 %copy-start = (f32[224,512]{1,0:T(8,128)S(1)}, f32[224,512]{1,0:T(8,128)}, u32[]{:S(2)}) copy-start(f32[224,512]{1,0:T(8,128)} %param.11) | copy-start | bytes 1376260
  163.6 318.9 %copy-start.1 = (f32[224,512]{1,0:T(8,128)S(1)}, f32[224,512]{1,0:T(8,128)}, u32[]{:S(2)}) copy-start(f32[224,512]{1,0:T(8,128)} %param.10) | copy-start | bytes 1376260
  483.7 8.4 %copy-start.2 = (f32[224,512]{1,0:T(8,128)}, f32[224,512]{1,0:T(8,128)S(1)}, u32[]{:S(2)}) copy-start(f32[224,512]{1,0:T(8,128)S(1)} %get-tuple-element.3) | copy-start | bytes 1376260
  483.7 8.3 %copy-start.3 = (f32[224,512]{1,0:T(8,128)}, f32[224,512]{1,0:T(8,128)S(1)}, u32[]{:S(2)}) copy-start(f32[224,512]{1,0:T(8,128)S(1)} %get-tuple-element.4) | copy-start | bytes 1376260
Sparse Core Ops, SparseCore 0:
  9.6 84.8 all-gather.1
  163.8 318.6 reduce-scatter.1
